TPU v7x, 32 devices: a whole 2x2x4 slice. The times are simulated.
32 devices in a mesh: edge: 8 (over y, x, core), feat: 4 (over z).
Axes of the slice: x: 2, y: 2, z: 4, core: 2. Of those that a mesh axis runs over, the one named last changes fastest.
Arguments:
- node_latents: bfloat16 [4, 4096, 256], P('feat', 'edge'), may hold values from -6 to 6
- edge_latents: bfloat16 [4, 32768, 256], P('feat', 'edge'), may hold values from -6 to 6
- senders: int32 [32768], P('edge'), may hold values from 0 to 4095, as said below
- receivers: int32 [32768], P('edge'), may hold values from 0 to 4095, as said below
- regions: int32 [32768], P('edge'), may hold values from 0 to 23
- forced: int32 [4096], P('edge'), may hold values 0 or 1
- params: float32 [1824, 256], P('feat'), may hold values from -1.5 to 1.5, as said below
- first_moment: float32 [1824, 256], P('feat'), may hold values from -0.34 to 0.34
- second_moment: float32 [1824, 256], P('feat'), may hold values from 0.004 to 0.22
- averaged: float32 [1824, 256], P('feat'), may hold values from -1.7 to 1.7
- step: int32 [1], replicated, may hold values from 1 to 20
- cotangent: float32 [4, 4096, 256], P('feat', 'edge'), may hold values from -6 to 6
Outputs:
- new_latents: float32 [4, 4096, 256], P('feat', 'edge')
- grad_latents: float32 [4, 4096, 256], P('feat', 'edge')
- grad_edges: bfloat16 [4, 32768, 256], P('feat', 'edge')
- new_first: float32 [1824, 256], P('feat')
- new_second: float32 [1824, 256], P('feat')
- new_params: float32 [1824, 256], P('feat')
- new_average: float32 [1824, 256], P('feat')
- grad_norm: float32 [1], replicated
- vector_grads: float32 [8, 256], replicated
Inputs may be any that keep to these rules, and one draw needn't show every extreme that they name: `senders`: nodes are numbered so that node block b is nodes b * 512 to (b + 1) * 512 - 1. Edge k lies in edge block e = k // 4096; its sender lies in node block e - 1, e or e + 1, taken cyclically over the 4096 nodes. `receivers`: the receiver of edge k lies in node block e - 1, e or e + 1 of its edge block e = k // 4096, taken cyclically. `params`: parameters scaled by fan-in; gains near one.
All inputs are finite; a program needn't handle non-finite values. No bound on the sum of `forced` on one device may be relied on, other than what follows from the above.
Results may differ from a plain program's by a relative error of at most 0.0039.
The roundings to bfloat16 on the way count: a program that leaves them out, or rounds other values in their place, can miss the bound.
Values may be sent and summed in bfloat16 or wider, within the bound.
No kernel may reach another device: no remote copies, remote signals or barrier semaphores. Data moves between devices by JAX's collectives and lax.ppermute only.
A program may use at most 128 MiB of HBM per device.

v0:
```python
import jax
import jax.numpy as jnp
from jax import lax
from jax.sharding import PartitionSpec as P

NORM_EPS = 1e-05
MAX_NORM = 512.0
RATE = 0.05
BETA_ONE = 0.9
BETA_TWO = 0.95
ADAM_EPS = 1e-08
WEIGHT_DECAY = 0.1
AVERAGE_DECAY = 0.999


def padded(cells, sides, width):
    for axis, dim in sides:
        count = lax.axis_size(axis)
        head = lax.slice_in_dim(cells, 0, width, axis=dim)
        tail = lax.slice_in_dim(cells, cells.shape[dim] - width, cells.shape[dim], axis=dim)
        cells = jnp.concatenate(
            [
                lax.ppermute(tail, axis, [(i, (i + 1) % count) for i in range(count)]),
                cells,
                lax.ppermute(head, axis, [((i + 1) % count, i) for i in range(count)]),
            ],
            axis=dim,
        )
    return cells


def passed_along(value, axis, steps):
    count = lax.axis_size(axis)
    pairs = [(source, (source + steps) % count) for source in range(count)]
    return lax.ppermute(value, axis, pairs)


def product(left, right):
    return jnp.dot(left, right, preferred_element_type=jnp.float32)


def outer_product(left, right):
    return lax.dot_general(
        left, right, (((0,), (0,)), ((), ())), preferred_element_type=jnp.float32
    )


def product_transposed(left, right):
    return lax.dot_general(
        left, right, (((1,), (1,)), ((), ())), preferred_element_type=jnp.float32
    )


def pick_rows(table, indices):
    return jnp.take(table, indices, axis=0)


def add_rows(values, indices, rows):
    return jax.ops.segment_sum(values, indices, num_segments=rows)


def normalized(values):
    center = values - jnp.mean(values, axis=-1, keepdims=True)
    spread = jnp.mean(center * center, axis=-1, keepdims=True)
    inverse = lax.rsqrt(spread + NORM_EPS)
    return (center * inverse, inverse)


def layer_norm(values, gain, shift):
    unit, inverse = normalized(values)
    return unit * gain + shift


def norm_backward(values, gain, upstream):
    unit, inverse = normalized(values)
    scaled = upstream * gain
    inner = (
        scaled
        - jnp.mean(scaled, axis=-1, keepdims=True)
        - unit * jnp.mean(scaled * unit, axis=-1, keepdims=True)
    )
    return (inverse * inner, jnp.sum(upstream * unit, axis=0), jnp.sum(upstream, axis=0))


def silu_slope(values):
    sigma = jax.nn.sigmoid(values)
    return sigma * (1.0 + values * (1.0 - sigma))


def neighbourhood(latents):
    return padded(latents, (("edge", 0),), latents.shape[0])


def on_device(
    node_latents,
    edge_latents,
    senders,
    receivers,
    regions,
    forced,
    params,
    first_moment,
    second_moment,
    averaged,
    step,
    cotangent,
):
    latents = node_latents[0]
    edges = edge_latents[0]
    upstream = cotangent[0]
    width = latents.shape[1]
    node_rows = latents.shape[0]
    total_nodes = node_rows * lax.axis_size("edge")
    lowest = (lax.axis_index("edge") - 1) * node_rows
    send_local = jnp.mod(senders - lowest, total_nodes)
    recv_local = jnp.mod(receivers - lowest, total_nodes)
    weights = lax.all_gather(params.astype(jnp.bfloat16), "feat", axis=0, tiled=True)
    first = weights[0 : 3 * width]
    second = weights[3 * width : 4 * width]
    node_first = weights[4 * width : 6 * width]
    node_second = weights[6 * width : 7 * width]
    vectors = weights[7 * width : 7 * width + 8].astype(jnp.float32)
    table = weights[7 * width + 8 :]
    region_onehot = jax.nn.one_hot(regions, table.shape[0], dtype=jnp.bfloat16)
    near_nodes = neighbourhood(latents)
    from_send = pick_rows(near_nodes, send_local)
    from_recv = pick_rows(near_nodes, recv_local)
    pre = product(from_send, first[0:width]) + product(from_recv, first[width : 2 * width])
    pre = (
        pre
        + product(edges, first[2 * width : 3 * width])
        + vectors[0]
        + product(region_onehot, table)
    )
    hidden = jax.nn.silu(pre).astype(jnp.bfloat16)
    inner = product(hidden, second) + vectors[1]
    from_send, from_recv, pre, hidden, inner = (from_send, from_recv, pre, hidden, inner)
    messages = layer_norm(inner, vectors[2], vectors[3])
    partial_value = add_rows(messages, recv_local, 3 * node_rows)
    from_below = passed_along(partial_value[2 * node_rows :], "edge", 1)
    from_above = passed_along(partial_value[0:node_rows], "edge", -1)
    aggregate = (partial_value[node_rows : 2 * node_rows] + from_below + from_above).astype(
        jnp.bfloat16
    )
    pre_node = (
        product(latents, node_first[0:width])
        + product(aggregate, node_first[width : 2 * width])
        + vectors[4]
    )
    hidden_node = jax.nn.silu(pre_node).astype(jnp.bfloat16)
    inner_node = product(hidden_node, node_second) + vectors[5]
    update = layer_norm(inner_node, vectors[6], vectors[7])
    keep = (1 - forced).astype(jnp.float32)[:, None]
    new_latents = latents.astype(jnp.float32) + keep * update
    d_update = upstream * keep
    d_inner_node, d_gain_node, d_shift_node = norm_backward(inner_node, vectors[6], d_update)
    d_inner_node = d_inner_node.astype(jnp.bfloat16)
    g_node_second = outer_product(hidden_node, d_inner_node)
    d_bias_node_second = jnp.sum(d_inner_node.astype(jnp.float32), axis=0)
    d_pre_node = (product_transposed(d_inner_node, node_second) * silu_slope(pre_node)).astype(
        jnp.bfloat16
    )
    g_node_first = jnp.concatenate(
        [outer_product(latents, d_pre_node), outer_product(aggregate, d_pre_node)], axis=0
    )
    d_bias_node_first = jnp.sum(d_pre_node.astype(jnp.float32), axis=0)
    d_from_nodes = product_transposed(d_pre_node, node_first[0:width])
    d_aggregate = product_transposed(d_pre_node, node_first[width : 2 * width]).astype(jnp.bfloat16)
    near_back = padded(d_aggregate, (("edge", 0),), node_rows)
    d_messages = pick_rows(near_back, recv_local).astype(jnp.float32)
    d_inner, d_gain_edge, d_shift_edge = norm_backward(inner, vectors[2], d_messages)
    d_inner = d_inner.astype(jnp.bfloat16)
    g_second = outer_product(hidden, d_inner)
    d_bias_second = jnp.sum(d_inner.astype(jnp.float32), axis=0)
    d_pre = (product_transposed(d_inner, second) * silu_slope(pre)).astype(jnp.bfloat16)
    g_first = jnp.concatenate(
        [
            outer_product(from_send, d_pre),
            outer_product(from_recv, d_pre),
            outer_product(edges, d_pre),
        ],
        axis=0,
    )
    d_bias_first = jnp.sum(d_pre.astype(jnp.float32), axis=0)
    g_table = outer_product(region_onehot, d_pre)
    d_send = product_transposed(d_pre, first[0:width])
    d_recv = product_transposed(d_pre, first[width : 2 * width])
    grad_edges = product_transposed(d_pre, first[2 * width : 3 * width]).astype(jnp.bfloat16)
    node_partial = add_rows(d_send, send_local, 3 * node_rows) + add_rows(
        d_recv, recv_local, 3 * node_rows
    )
    grads_below = passed_along(
        node_partial[2 * node_rows :].astype(jnp.bfloat16), "edge", 1
    ).astype(jnp.float32)
    grads_above = passed_along(node_partial[0:node_rows].astype(jnp.bfloat16), "edge", -1).astype(
        jnp.float32
    )
    d_nodes = node_partial[node_rows : 2 * node_rows] + grads_below + grads_above
    grad_latents = upstream + d_from_nodes + d_nodes
    vector_rows = jnp.stack(
        [
            d_bias_first,
            d_bias_second,
            d_gain_edge,
            d_shift_edge,
            d_bias_node_first,
            d_bias_node_second,
            d_gain_node,
            d_shift_node,
        ],
        axis=0,
    )
    local_grad = jnp.concatenate(
        [g_first, g_second, g_node_first, g_node_second, vector_rows, g_table], axis=0
    )
    share = params.shape[0]
    summed = lax.psum(local_grad, ("edge", "feat"))
    owned = lax.dynamic_slice_in_dim(summed, lax.axis_index("feat") * share, share, 0)
    rows_here = lax.axis_index("feat") * share + lax.broadcasted_iota(jnp.int32, (8, share), 1)
    wanted = 7 * width + lax.broadcasted_iota(jnp.int32, (8, share), 0)
    select = (rows_here == wanted).astype(jnp.float32)
    vector_piece = jnp.dot(
        select, owned, precision=lax.Precision.HIGHEST, preferred_element_type=jnp.float32
    )
    squares, vector_total = lax.psum((jnp.sum(owned * owned), vector_piece), "feat")
    grad_norm = jnp.sqrt(squares)
    factor = jnp.minimum(1.0, MAX_NORM / (grad_norm + 1e-06))
    clipped = owned * factor
    vector_grads = vector_total * factor
    new_first = BETA_ONE * first_moment + (1.0 - BETA_ONE) * clipped
    new_second = BETA_TWO * second_moment + (1.0 - BETA_TWO) * clipped * clipped
    count_steps = step[0].astype(jnp.float32)
    first_hat = new_first / (1.0 - jnp.power(BETA_ONE, count_steps))
    second_hat = new_second / (1.0 - jnp.power(BETA_TWO, count_steps))
    new_params = params - RATE * (
        first_hat / (jnp.sqrt(second_hat) + ADAM_EPS) + WEIGHT_DECAY * params
    )
    decay_now = jnp.minimum(AVERAGE_DECAY, (1.0 + count_steps) / (10.0 + count_steps))
    new_average = decay_now * averaged + (1.0 - decay_now) * new_params
    return (
        new_latents[None],
        grad_latents[None],
        grad_edges[None],
        new_first,
        new_second,
        new_params,
        new_average,
        grad_norm.reshape(1),
        vector_grads,
    )


def solution(mesh):
    placed = (
        P("feat", "edge", None),
        P("feat", "edge", None),
        P("edge"),
        P("edge"),
        P("edge"),
        P("edge"),
        P("feat", None),
        P("feat", None),
        P("feat", None),
        P("feat", None),
        P(),
        P("feat", "edge", None),
    )
    return jax.shard_map(
        on_device,
        mesh=mesh,
        in_specs=placed,
        out_specs=(
            P("feat", "edge", None),
            P("feat", "edge", None),
            P("feat", "edge", None),
            P("feat", None),
            P("feat", None),
            P("feat", None),
            P("feat", None),
            P(),
            P(),
        ),
        check_vma=False,
    )
```

profile of v0, /device:TPU:0, one launch (start us, length us, event | category | flops | bytes accessed | tf_op | source)
XLA Modules:
  0.0 374.1 jit_solution(12631992785596046417)
XLA Ops:
  13.8 22.2 %all_gather.3 = bf16[1824,256]{1,0:T(8,128)(2,1)S(1)} all-gather(bf16[456,256]{1,0:T(8,128)(2,1)S(1)} %convert_element_type.71), channel_id=1, replica_groups=mesh['edge'=8,'feat'=4] {'feat'}, dimensions={0}, use_global_device_ids=true | all-gather | bytes 1167360 | tf_op jit(solution)/shard_map/all_gather | solution.py:117
  39.3 17.0 %gather_fusion = bf16[4096,256]{1,0:T(8,128)(2,1)} fusion(bf16[1536,256]{1,0:T(8,128)(2,1)S(1)} %copy.43, s32[4096]{0:T(1024)S(1)} %fusion.66), kind=kCustom, calls=%fused_computation.clone | custom fusion | bytes 4210688 | tf_op jit(solution)/shard_map/jit(_take)/gather | solution.py:55
  56.4 16.9 %gather_fusion.1 = bf16[4096,256]{1,0:T(8,128)(2,1)} fusion(bf16[1536,256]{1,0:T(8,128)(2,1)S(1)} %copy.43, s32[4096]{0:T(1024)S(1)} %fusion.67), kind=kCustom, calls=%fused_computation.1.clone | custom fusion | bytes 4210688 | tf_op jit(solution)/shard_map/jit(_take)/gather | solution.py:55
  73.3 4.0 %fusion.20 = f32[4096,256]{1,0:T(8,128)S(1)} fusion(bf16[4096,256]{1,0:T(8,128)(2,1)} %gather_fusion, pred[4096]{0:T(1024)(128)(4,1)S(1)} %get-tuple-element.86, bf16[1824,256]{1,0:T(8,128)(2,1)} %copy-done.10), kind=kOutput, calls=%fused_computation.49 | convolution fusion | flops 537919488 | bytes 6426624 | tf_op jit(solution)/shard_map/dot_general | solution.py:39
  80.7 4.0 %multiply_convert_fusion = (bf16[4096,256]{1,0:T(8,128)(2,1)S(1)}, f32[4096,256]{1,0:T(8,128)}) fusion(f32[4096,256]{1,0:T(8,128)S(1)} %fusion.3, bf16[1824,256]{1,0:T(8,128)(2,1)} %copy-done.10, s32[4096]{0:T(1024)S(1)} %copy-done.23), kind=kOutput, calls=%fused_computation.30 | convolution fusion | flops 56721408 | bytes 10514432 | tf_op jit(solution)/shard_map/dot_general | solution.py:39
  91.2 5.6 %copy.45 = f32[4096,256]{1,0:T(8,128)} copy(f32[4096,256]{0,1:T(8,128)} %multiply_add_fusion) | data formatting | bytes 8388608 | tf_op jit(solution)/shard_map/add | solution.py:71
  96.8 24.1 %scatter_custom_fusion = f32[1536,256]{1,0:T(8,128)} fusion(s32[4096]{0:T(1024)S(1)} %get-tuple-element.58, f32[4096,256]{1,0:T(8,128)} %copy.45, f32[]{:T(128)} %constant.42.clone.1), kind=kCustom, calls=%fused_computation.57 | custom fusion | flops 1048576 | bytes 1573376 | tf_op jit(solution)/shard_map/scatter-add | solution.py:59
  128.8 8.7 %collective-permute-done.2 = f32[512,256]{1,0:T(8,128)S(1)} collective-permute-done((f32[512,256]{1,0:T(8,128)}, f32[512,256]{1,0:T(8,128)S(1)}, u32[]{:S(2)}, u32[]{:S(2)}) %collective-permute-start.2) | collective-permute-done | bytes 524320 | tf_op jit(solution)/shard_map/ppermute | solution.py:35
  152.0 4.5 %collective-permute-done.4 = bf16[512,256]{1,0:T(8,128)(2,1)S(1)} collective-permute-done((bf16[512,256]{1,0:T(8,128)(2,1)S(1)}, bf16[512,256]{1,0:T(8,128)(2,1)S(1)}, u32[]{:S(2)}, u32[]{:S(2)}) %collective-permute-start.4) | collective-permute-done | bytes 262176 | tf_op jit(solution)/shard_map/ppermute | solution.py:23
  156.6 16.9 %gather_fusion.2 = bf16[4096,256]{1,0:T(8,128)(2,1)} fusion(bf16[1536,256]{1,0:T(8,128)(2,1)S(1)} %pad_maximum_fusion.1, s32[4096]{0:T(1024)S(1)} %fusion.67), kind=kCustom, calls=%fused_computation.2.clone | custom fusion | bytes 4210688 | tf_op jit(solution)/shard_map/jit(_take)/gather | solution.py:55
  173.5 4.1 %copy.48 = bf16[4096,256]{0,1:T(8,128)(2,1)} copy(bf16[4096,256]{1,0:T(8,128)(2,1)} %gather_fusion.2) | data formatting | bytes 4194304 | tf_op jit(solution)/shard_map/jit(_take)/gather | solution.py:55
  177.6 5.3 %fusion.10 = (f32[256]{0:T(256)S(1)}, f32[4096]{0:T(1024)S(1)}, f32[4096]{0:T(1024)S(1)}, f32[256]{0:T(256)S(1)}) fusion(f32[4096,256]{0,1:T(8,128)} %copy-done.1, f32[4096]{0:T(1024)S(1)} %add_rsqrt_fusion, f32[4096]{0:T(1024)S(1)} %broadcast_multiply_fusion.2, bf16[4096,256]{0,1:T(8,128)(2,1)} %copy.48, pred[4096]{0:T(1024)(128)(4,1)S(1)} %get-tuple-element.57, ...), kind=kLoop, calls=%fused_computation.25 | loop fusion | flops 11525632 | bytes 6364160 | tf_op jit(solution)/shard_map/reduce_sum | solution.py:82
  187.6 3.0 convert_reduce_fusion.2
  197.1 3.6 fusion.53
  200.8 3.8 %fusion.56 = f32[4096,256]{1,0:T(8,128)} fusion(bf16[4096,256]{1,0:T(8,128)(2,1)S(1)} %get-tuple-element.83, bf16[1824,256]{1,0:T(8,128)(2,1)} %copy-done.10), kind=kOutput, calls=%fused_computation.106 | convolution fusion | flops 536870912 | bytes 6422528 | tf_op jit(solution)/shard_map/dot_general | solution.py:49
  204.6 10.1 %concatenate.11 = f32[1824,256]{1,0:T(8,128)} concatenate(f32[256,256]{1,0:T(8,128)} %fusion.19, f32[256,256]{1,0:T(8,128)} %fusion.21, f32[256,256]{1,0:T(8,128)} %fusion.16, f32[256,256]{1,0:T(8,128)} %fusion.84, f32[256,256]{1,0:T(8,128)S(1)} %copy-done.20, f32[256,256]{1,0:T(8,128)S(1)} %copy-done.19, f32[256,256]{1,0:T(8,128)S(1)} %copy-done.18, f32[1,256]{1,0:T(1,128)S(1)} %bitcast.104, ...), dimensions={0} | concatenate | bytes 3735552 | tf_op jit(solution)/shard_map/concatenate | solution.py:213
  214.7 24.0 %scatter_custom_fusion.2 = f32[1536,256]{1,0:T(8,128)} fusion(s32[4096]{0:T(1024)S(1)} %get-tuple-element.58, f32[4096,256]{1,0:T(8,128)} %fusion.53, f32[]{:T(128)} %constant.42.clone.1), kind=kCustom, calls=%fused_computation.53 | custom fusion | flops 1048576 | bytes 1573376 | tf_op jit(solution)/shard_map/scatter-add | solution.py:59
  238.8 3.1 copy.50
  241.9 24.0 %scatter_custom_fusion.1 = f32[1536,256]{1,0:T(8,128)} fusion(s32[4096]{0:T(1024)S(1)} %get-tuple-element.87, f32[4096,256]{1,0:T(8,128)} %fusion.56, f32[]{:T(128)} %constant.42.clone.1), kind=kCustom, calls=%fused_computation.55 | custom fusion | flops 1048576 | bytes 1573376 | tf_op jit(solution)/shard_map/scatter-add | solution.py:59
  265.9 3.1 copy.49
  269.0 3.4 fusion.78
  278.1 3.7 fusion.5
  283.5 61.5 %all-reduce.3.cloned.1.call-done = f32[1824,256]{1,0:T(8,128)} async-done(((f32[1824,256]{1,0:T(8,128)}), f32[1824,256]{1,0:T(8,128)}) %all-reduce.3.cloned.1.call-update) | async-done | bytes 1867792 | tf_op jit(solution)/shard_map/psum | solution.py:217
  349.6 12.4 %all-reduce = (f32[]{:T(128)}, f32[8,256]{1,0:T(8,128)S(1)}) all-reduce(f32[]{:T(128)} %multiply_reduce_fusion.4, f32[8,256]{1,0:T(8,128)} %fusion.38), channel_id=1, replica_groups=mesh['edge'=8,'feat'=4] {'feat'}, use_global_device_ids=true, to_apply=%region_21.23 | all-reduce | flops 2049 | bytes 16392 | tf_op jit(solution)/shard_map/psum | solution.py:225
  (122 shorter events, 67.8 us)
Async XLA Ops:
  7.2 71.8 %copy-start = (bf16[1,4096,256]{2,1,0:T(8,128)(2,1)S(1)}, bf16[1,4096,256]{2,1,0:T(8,128)(2,1)}, u32[]{:S(2)}) copy-start(bf16[1,4096,256]{2,1,0:T(8,128)(2,1)} %param.15) | copy-start | bytes 6291460
  7.2 337.8 %all-reduce.3.cloned.1.call-start = ((), (), s32[]{:S(2)}) async-start(), calls=%async_computation | async-start | bytes 3735552 | tf_op jit(solution)/shard_map/psum | solution.py:217
  8.5 28.5 %copy-start.14 = (bf16[1,512,256]{1,2,0:T(8,128)(2,1)}, bf16[1,512,256]{1,2,0:T(8,128)(2,1)S(1)}, u32[]{:S(2)}) copy-start(bf16[1,512,256]{1,2,0:T(8,128)(2,1)S(1)} %copy.42) | copy-start | bytes 786436
  8.5 28.5 %collective-permute-start = (bf16[512,256]{0,1:T(8,128)(2,1)S(1)}, bf16[512,256]{0,1:T(8,128)(2,1)S(1)}, u32[]{:S(2)}, u32[]{:S(2)}) collective-permute-start(bf16[512,256]{0,1:T(8,128)(2,1)S(1)} %bitcast.84), channel_id=1, source_target_pairs={{0,4},{4,8},{8,12},{12,16},{16,20},{20,24},{24,28},{28,0},{1,5},{5... | collective-permute-start | bytes 786440 | tf_op jit(solution)/shard_map/ppermute | solution.py:23
  9.0 28.0 %collective-permute-start.1 = (bf16[512,256]{0,1:T(8,128)(2,1)S(1)}, bf16[512,256]{0,1:T(8,128)(2,1)S(1)}, u32[]{:S(2)}, u32[]{:S(2)}) collective-permute-start(bf16[512,256]{0,1:T(8,128)(2,1)S(1)} %bitcast.85), channel_id=1, source_target_pairs={{4,0},{8,4},{12,8},{16,12},{20,16},{24,20},{28,24},{0,28},{5,1},{9... | collective-permute-start | bytes 786440 | tf_op jit(solution)/shard_map/ppermute | solution.py:25
  73.3 4.0 %copy-start.8 = (bf16[4096,256]{1,0:T(8,128)(2,1)S(1)}, bf16[4096,256]{1,0:T(8,128)(2,1)}, u32[]{:S(2)}) copy-start(bf16[4096,256]{1,0:T(8,128)(2,1)} %gather_fusion.1) | copy-start | bytes 6291460
  96.8 30.8 %copy-start.24 = (s32[512]{0:T(512)S(1)}, s32[512]{0:T(512)}, u32[]{:S(2)}) copy-start(s32[512]{0:T(512)} %param.19) | copy-start | bytes 6148
  96.8 30.8 %copy-start.13 = (bf16[1,512,256]{2,1,0:T(8,128)(2,1)S(1)}, bf16[1,512,256]{2,1,0:T(8,128)(2,1)}, u32[]{:S(2)}) copy-start(bf16[1,512,256]{2,1,0:T(8,128)(2,1)} %param.14) | copy-start | bytes 786436
  123.2 14.4 %collective-permute-start.2 = (f32[512,256]{1,0:T(8,128)}, f32[512,256]{1,0:T(8,128)S(1)}, u32[]{:S(2)}, u32[]{:S(2)}) collective-permute-start(f32[512,256]{1,0:T(8,128)} %get-tuple-element.61), channel_id=1, source_target_pairs={{0,4},{4,8},{8,12},{12,16},{16,20},{20,24},{24,28},{28,0},{1,5},{5... | collective-permute-start | bytes 1572872 | tf_op jit(solution)/shard_map/ppermute | solution.py:35
  123.2 15.2 %collective-permute-start.3 = (f32[512,256]{1,0:T(8,128)}, f32[512,256]{1,0:T(8,128)}, u32[]{:S(2)}, u32[]{:S(2)}) collective-permute-start(f32[512,256]{1,0:T(8,128)} %get-tuple-element.62), channel_id=1, source_target_pairs={{0,28},{4,0},{8,4},{12,8},{16,12},{20,16},{24,20},{28,24},{1,29},{... | collective-permute-start | bytes 1572872 | tf_op jit(solution)/shard_map/ppermute | solution.py:35
  146.0 10.5 %copy-start.11 = (bf16[512,256]{1,0:T(8,128)(2,1)}, bf16[512,256]{1,0:T(8,128)(2,1)S(1)}, u32[]{:S(2)}) copy-start(bf16[512,256]{1,0:T(8,128)(2,1)S(1)} %get-tuple-element.85) | copy-start | bytes 786436
  147.3 9.2 %collective-permute-start.4 = (bf16[512,256]{1,0:T(8,128)(2,1)S(1)}, bf16[512,256]{1,0:T(8,128)(2,1)S(1)}, u32[]{:S(2)}, u32[]{:S(2)}) collective-permute-start(bf16[512,256]{1,0:T(8,128)(2,1)S(1)} %convolution_convert_fusion.1), channel_id=1, source_target_pairs={{0,4},{4,8},{8,12},{12,16},{16,20},{20,24},{24,28},{28,0},{1,5},{5... | collective-permute-start | bytes 786440 | tf_op jit(solution)/shard_map/ppermute | solution.py:23
  147.4 9.1 %collective-permute-start.5 = (bf16[512,256]{1,0:T(8,128)(2,1)S(1)}, bf16[512,256]{1,0:T(8,128)(2,1)S(1)}, u32[]{:S(2)}, u32[]{:S(2)}) collective-permute-start(bf16[512,256]{1,0:T(8,128)(2,1)S(1)} %convolution_convert_fusion.1), channel_id=1, source_target_pairs={{4,0},{8,4},{12,8},{16,12},{20,16},{24,20},{28,24},{0,28},{5,1},{9... | collective-permute-start | bytes 786440 | tf_op jit(solution)/shard_map/ppermute | solution.py:25
  177.6 5.4 %copy-start.2 = (f32[4096,256]{0,1:T(8,128)S(1)}, f32[4096,256]{0,1:T(8,128)}, u32[]{:S(2)}) copy-start(f32[4096,256]{0,1:T(8,128)} %copy-done.1) | copy-start | bytes 12582916
  177.6 5.4 %copy-start.4 = (bf16[4096,256]{0,1:T(8,128)(2,1)S(1)}, bf16[4096,256]{0,1:T(8,128)(2,1)}, u32[]{:S(2)}) copy-start(bf16[4096,256]{0,1:T(8,128)(2,1)} %copy.48) | copy-start | bytes 6291460
  190.6 10.2 %copy-start.3 = (bf16[4096,256]{1,0:T(8,128)(2,1)}, bf16[4096,256]{1,0:T(8,128)(2,1)S(1)}, u32[]{:S(2)}) copy-start(bf16[4096,256]{1,0:T(8,128)(2,1)S(1)} %get-tuple-element.83) | copy-start | bytes 6291460
  200.8 3.8 %copy-start.19 = (f32[256,256]{1,0:T(8,128)S(1)}, f32[256,256]{1,0:T(8,128)}, u32[]{:S(2)}) copy-start(f32[256,256]{1,0:T(8,128)} %fusion.85) | copy-start | bytes 786436
  200.8 3.8 %copy-start.20 = (f32[256,256]{1,0:T(8,128)S(1)}, f32[256,256]{1,0:T(8,128)}, u32[]{:S(2)}) copy-start(f32[256,256]{1,0:T(8,128)} %convolution_bitcast_fusion) | copy-start | bytes 786436
  269.0 8.2 %copy-start.16 = (f32[1,512,256]{1,2,0:T(8,128)S(1)}, f32[1,512,256]{1,2,0:T(8,128)}, u32[]{:S(2)}) copy-start(f32[1,512,256]{1,2,0:T(8,128)} %get-tuple-element.65) | copy-start | bytes 1572868
  273.2 8.8 %collective-permute-start.6 = (bf16[512,256]{0,1:T(8,128)(2,1)}, bf16[512,256]{0,1:T(8,128)(2,1)S(1)}, u32[]{:S(2)}, u32[]{:S(2)}) collective-permute-start(bf16[512,256]{0,1:T(8,128)(2,1)} %get-tuple-element.63), channel_id=1, source_target_pairs={{0,4},{4,8},{8,12},{12,16},{16,20},{20,24},{24,28},{28,0},{1,5},{5... | collective-permute-start | bytes 786440 | tf_op jit(solution)/shard_map/ppermute | solution.py:35
  273.2 8.8 %collective-permute-start.7 = (bf16[512,256]{0,1:T(8,128)(2,1)}, bf16[512,256]{0,1:T(8,128)(2,1)}, u32[]{:S(2)}, u32[]{:S(2)}) collective-permute-start(bf16[512,256]{0,1:T(8,128)(2,1)} %get-tuple-element.64), channel_id=1, source_target_pairs={{0,28},{4,0},{8,4},{12,8},{16,12},{20,16},{24,20},{28,24},{1,29},{... | collective-permute-start | bytes 786440 | tf_op jit(solution)/shard_map/ppermute | solution.py:35
  278.1 3.9 %copy-start.12 = (bf16[512,256]{1,0:T(8,128)(2,1)S(1)}, bf16[512,256]{1,0:T(8,128)(2,1)}, u32[]{:S(2)}) copy-start(bf16[512,256]{1,0:T(8,128)(2,1)} %copy-done.11) | copy-start | bytes 786436
  283.5 79.8 %copy-start.17 = (f32[456,256]{1,0:T(8,128)S(1)}, f32[456,256]{1,0:T(8,128)}, u32[]{:S(2)}) copy-start(f32[456,256]{1,0:T(8,128)} %param.20) | copy-start | bytes 1400836
  283.5 79.8 %copy-start.22 = (f32[456,256]{1,0:T(8,128)S(1)}, f32[456,256]{1,0:T(8,128)}, u32[]{:S(2)}) copy-start(f32[456,256]{1,0:T(8,128)} %param.23) | copy-start | bytes 1400836
  (11 other events, 23.9 us)
Sparse Core Ops, SparseCore 0:
  214.8 130.0 all-reduce.2
where the time goes:
time: 375 us; the launch traced here: 374 us
  other arithmetic  98.5 us (26%)
  local copies, waits for them, and re-layouts  90 us (24%)
  waiting for transfers between devices  74.9 us (20%)
  matrix products  47.4 us (13%)
  blocking collectives  34.6 us (9%)
  between operations  17.2 us (5%)
  starting transfers between devices  11.5 us (3%)
    scatter-add x3, other arithmetic, add_rows(): return jax.ops.segment_sum(values, indices, num_segments=rows)  72.2 us
    psum x1, waiting for transfers between devices, on_device(): summed = lax.psum(local_grad, ('edge', 'feat'))  61.5 us
    gather x4, local copies, waits for them, and re-layouts, pick_rows(): return jnp.take(table, indices, axis=0)  55 us
    all_gather x1, blocking collectives, on_device(): lax.all_gather(params.astype(jnp.bfloat16), 'feat', axis=0, tiled=True)  22.2 us
    dot_general x7, matrix products, product_transposed(): lax.dot_general(left, right, (((1,), (1,)), ((), ())), preferred_element_...  18 us
    dot_general x8, matrix products, product(): return jnp.dot(left, right, preferred_element_type=jnp.float32)  16.7 us
    psum x1, blocking collectives, on_device(): lax.psum((jnp.sum(owned * owned), vector_piece), 'feat')  12.4 us
    dot_general x8, matrix products, outer_product(): lax.dot_general(left, right, (((0,), (0,)), ((), ())), preferred_element_...  10.7 us
  transfers between devices with their start and end apart: 9, of which 4 were waited for; matrix products, arithmetic and copies ran while one was open for 19% of the time, Pallas kernels for 0%

commit v1 on v0

--- a/solution.py
+++ b/solution.py
@@ -214,7 +214,7 @@
         [g_first, g_second, g_node_first, g_node_second, vector_rows, g_table], axis=0
     )
     share = params.shape[0]
-    summed = lax.psum(local_grad, ("edge", "feat"))
+    summed = jnp.sum(lax.all_gather(local_grad, ("edge", "feat")), axis=0)
     owned = lax.dynamic_slice_in_dim(summed, lax.axis_index("feat") * share, share, 0)
     rows_here = lax.axis_index("feat") * share + lax.broadcasted_iota(jnp.int32, (8, share), 1)
     wanted = 7 * width + lax.broadcasted_iota(jnp.int32, (8, share), 0)

time: 375 us -> 586 us (1.56); the launches traced: 374 us -> 577 us
  waiting for transfers between devices: 74.9 us -> 262 us
  other arithmetic: 98.5 us -> 118 us
    all_gather x0 -> x1, waiting for transfers between devices: none -> 241 us  [on_device(): summed = jnp.sum(lax.all_gather(local_grad, ('edge', 'feat')), axis=0)]
    psum x1 -> x0, waiting for transfers between devices: 61.5 us -> none  [on_device(): summed = lax.psum(local_grad, ('edge', 'feat'))]
    reduce_sum x0 -> x1, other arithmetic: none -> 20.2 us  [on_device(): summed = jnp.sum(lax.all_gather(local_grad, ('edge', 'feat')), axis=0)]
    ppermute x4, waiting for transfers between devices: 8.93 us -> 17.3 us  [passed_along(): return lax.ppermute(value, axis, pairs)]
  transfers between devices with their start and end apart: 9 -> 9, of which waited for: 4 -> 7; matrix products, arithmetic and copies ran while one was open for 19% -> 14% of each run, Pallas kernels for 0% -> 0%
where the time goes in v1:
time: 586 us; the launch traced here: 577 us
  waiting for transfers between devices  262 us (45%)
  other arithmetic  118 us (20%)
  local copies, waits for them, and re-layouts  90.1 us (15%)
  matrix products  48.7 us (8%)
  blocking collectives  32.2 us (5%)
  between operations  17.3 us (3%)
  starting transfers between devices  8.29 us (1%)
    all_gather x1, waiting for transfers between devices, on_device(): summed = jnp.sum(lax.all_gather(local_grad, ('edge', 'feat')), axis=0)  241 us
    scatter-add x3, other arithmetic, add_rows(): return jax.ops.segment_sum(values, indices, num_segments=rows)  72.3 us
    gather x4, local copies, waits for them, and re-layouts, pick_rows(): return jnp.take(table, indices, axis=0)  55 us
    all_gather x1, blocking collectives, on_device(): lax.all_gather(params.astype(jnp.bfloat16), 'feat', axis=0, tiled=True)  21.5 us
    reduce_sum x1, other arithmetic, on_device(): summed = jnp.sum(lax.all_gather(local_grad, ('edge', 'feat')), axis=0)  20.2 us
    dot_general x7, matrix products, product_transposed(): lax.dot_general(left, right, (((1,), (1,)), ((), ())), preferred_element_...  19.3 us
    ppermute x4, waiting for transfers between devices, passed_along(): return lax.ppermute(value, axis, pairs)  17.3 us
    dot_general x8, matrix products, product(): return jnp.dot(left, right, preferred_element_type=jnp.float32)  16.7 us
  transfers between devices with their start and end apart: 9, of which 7 were waited for; matrix products, arithmetic and copies ran while one was open for 14% of the time, Pallas kernels for 0%

profile of v1, /device:TPU:0, one launch (start us, length us, event | category | flops | bytes accessed | tf_op | source)
XLA Modules:
  0.0 577.3 jit_solution(6067547649934212919)
XLA Ops:
  8.5 3.4 collective-permute-start.1
  12.9 21.5 %all_gather.9 = bf16[1824,256]{1,0:T(8,128)(2,1)S(1)} all-gather(bf16[456,256]{1,0:T(8,128)(2,1)S(1)} %convert_element_type.71), channel_id=1, replica_groups=mesh['edge'=8,'feat'=4] {'feat'}, dimensions={0}, use_global_device_ids=true | all-gather | bytes 1167360 | tf_op jit(solution)/shard_map/all_gather | solution.py:117
  37.9 17.0 %gather_fusion = bf16[4096,256]{1,0:T(8,128)(2,1)} fusion(bf16[1536,256]{1,0:T(8,128)(2,1)S(1)} %copy.43, s32[4096]{0:T(1024)S(1)} %fusion.66), kind=kCustom, calls=%fused_computation.clone | custom fusion | bytes 4210688 | tf_op jit(solution)/shard_map/jit(_take)/gather | solution.py:55
  54.9 16.9 %gather_fusion.1 = bf16[4096,256]{1,0:T(8,128)(2,1)} fusion(bf16[1536,256]{1,0:T(8,128)(2,1)S(1)} %copy.43, s32[4096]{0:T(1024)S(1)} %fusion.67), kind=kCustom, calls=%fused_computation.1.clone | custom fusion | bytes 4210688 | tf_op jit(solution)/shard_map/jit(_take)/gather | solution.py:55
  71.8 4.0 fusion.20
  79.3 4.0 multiply_convert_fusion
  89.8 5.6 copy.45
  95.4 24.1 %scatter_custom_fusion = f32[1536,256]{1,0:T(8,128)} fusion(s32[4096]{0:T(1024)S(1)} %get-tuple-element.58, f32[4096,256]{1,0:T(8,128)} %copy.45, f32[]{:T(128)} %constant.42.clone.1), kind=kCustom, calls=%fused_computation.57 | custom fusion | flops 1048576 | bytes 1573376 | tf_op jit(solution)/shard_map/scatter-add | solution.py:59
  125.4 9.2 %collective-permute-done.3 = f32[512,256]{1,0:T(8,128)S(1)} collective-permute-done((f32[512,256]{1,0:T(8,128)}, f32[512,256]{1,0:T(8,128)S(1)}, u32[]{:S(2)}, u32[]{:S(2)}) %collective-permute-start.3) | collective-permute-done | bytes 524320 | tf_op jit(solution)/shard_map/ppermute | solution.py:35
  152.8 16.9 %gather_fusion.2 = bf16[4096,256]{1,0:T(8,128)(2,1)} fusion(bf16[1536,256]{1,0:T(8,128)(2,1)S(1)} %pad_maximum_fusion.1, s32[4096]{0:T(1024)S(1)} %fusion.67), kind=kCustom, calls=%fused_computation.2.clone | custom fusion | bytes 4210688 | tf_op jit(solution)/shard_map/jit(_take)/gather | solution.py:55
  169.8 4.1 copy.48
  173.9 5.3 fusion.10
  193.3 10.1 %concatenate.11 = f32[1824,256]{1,0:T(8,128)} concatenate(f32[256,256]{1,0:T(8,128)} %fusion.19, f32[256,256]{1,0:T(8,128)} %fusion.21, f32[256,256]{1,0:T(8,128)} %fusion.16, f32[256,256]{1,0:T(8,128)} %fusion.84, f32[256,256]{1,0:T(8,128)S(1)} %copy-done.18, f32[256,256]{1,0:T(8,128)S(1)} %copy-done.19, f32[256,256]{1,0:T(8,128)S(1)} %copy-done.20, f32[1,256]{1,0:T(1,128)S(1)} %bitcast.106, ...), dimensions={0} | concatenate | bytes 3735552 | tf_op jit(solution)/shard_map/concatenate | solution.py:213
  204.0 4.4 fusion.56
  208.4 24.2 %scatter_custom_fusion.1 = f32[1536,256]{1,0:T(8,128)} fusion(s32[4096]{0:T(1024)S(1)} %get-tuple-element.87, f32[4096,256]{1,0:T(8,128)} %fusion.56, f32[]{:T(128)} %constant.42.clone.1), kind=kCustom, calls=%fused_computation.55 | custom fusion | flops 1048576 | bytes 1573376 | tf_op jit(solution)/shard_map/scatter-add | solution.py:59
  235.7 4.4 fusion.53
  240.1 24.0 %scatter_custom_fusion.2 = f32[1536,256]{1,0:T(8,128)} fusion(s32[4096]{0:T(1024)S(1)} %get-tuple-element.58, f32[4096,256]{1,0:T(8,128)} %fusion.53, f32[]{:T(128)} %constant.42.clone.1), kind=kCustom, calls=%fused_computation.53 | custom fusion | flops 1048576 | bytes 1573376 | tf_op jit(solution)/shard_map/scatter-add | solution.py:59
  264.1 3.2 copy.50
  267.3 3.4 fusion.78
  274.9 3.7 fusion.5
  278.6 6.1 %collective-permute-done.7 = bf16[512,256]{0,1:T(8,128)(2,1)S(1)} collective-permute-done((bf16[512,256]{0,1:T(8,128)(2,1)}, bf16[512,256]{0,1:T(8,128)(2,1)S(1)}, u32[]{:S(2)}, u32[]{:S(2)}) %collective-permute-start.7) | collective-permute-done | bytes 262176 | tf_op jit(solution)/shard_map/ppermute | solution.py:35
  288.0 241.3 %all-gather.3.cloned.1.call-done = f32[58368,256]{1,0:T(8,128)} async-done(((f32[1824,256]{1,0:T(8,128)}), f32[58368,256]{1,0:T(8,128)}) %all-gather.3.cloned.1.call-update) | async-done | bytes 59768848 | tf_op jit(solution)/shard_map/all_gather | solution.py:217
  529.4 20.2 %reduce_sum.194 = f32[1824,256]{1,0:T(8,128)} reduce(f32[32,1824,256]{2,1,0:T(8,128)} %bitcast.85, f32[]{:T(128)} %constant.42.clone.1), dimensions={0}, to_apply=%region_19.21 | reduce | flops 14475264 | bytes 61636612 | tf_op jit(solution)/shard_map/reduce_sum | solution.py:217
  554.3 10.7 %all-reduce = (f32[]{:T(128)}, f32[8,256]{1,0:T(8,128)S(1)}) all-reduce(f32[]{:T(128)} %multiply_reduce_fusion.4, f32[8,256]{1,0:T(8,128)} %fusion.38), channel_id=1, replica_groups=mesh['edge'=8,'feat'=4] {'feat'}, use_global_device_ids=true, to_apply=%region_21.23 | all-reduce | flops 2049 | bytes 16392 | tf_op jit(solution)/shard_map/psum | solution.py:225
  (127 shorter events, 72.1 us)
Async XLA Ops:
  7.2 70.4 %copy-start = (bf16[1,4096,256]{2,1,0:T(8,128)(2,1)S(1)}, bf16[1,4096,256]{2,1,0:T(8,128)(2,1)}, u32[]{:S(2)}) copy-start(bf16[1,4096,256]{2,1,0:T(8,128)(2,1)} %param.15) | copy-start | bytes 6291460
  7.2 28.2 %copy-start.24 = (s32[4096]{0:T(1024)S(1)}, s32[4096]{0:T(1024)}, u32[]{:S(2)}) copy-start(s32[4096]{0:T(1024)} %param.17) | copy-start | bytes 49156
  7.2 28.2 %copy-start.25 = (s32[4096]{0:T(1024)S(1)}, s32[4096]{0:T(1024)}, u32[]{:S(2)}) copy-start(s32[4096]{0:T(1024)} %param.16) | copy-start | bytes 49156
  7.2 522.2 %all-gather.3.cloned.1.call-start = ((), (), s32[]{:S(2)}) async-start(), calls=%async_computation | async-start | bytes 61636608 | tf_op jit(solution)/shard_map/all_gather | solution.py:217
  8.5 27.0 %copy-start.14 = (bf16[1,512,256]{1,2,0:T(8,128)(2,1)}, bf16[1,512,256]{1,2,0:T(8,128)(2,1)S(1)}, u32[]{:S(2)}) copy-start(bf16[1,512,256]{1,2,0:T(8,128)(2,1)S(1)} %copy.42) | copy-start | bytes 786436
  8.5 27.0 %collective-permute-start.1 = (bf16[512,256]{0,1:T(8,128)(2,1)S(1)}, bf16[512,256]{0,1:T(8,128)(2,1)S(1)}, u32[]{:S(2)}, u32[]{:S(2)}) collective-permute-start(bf16[512,256]{0,1:T(8,128)(2,1)S(1)} %bitcast.86), channel_id=1, source_target_pairs={{4,0},{8,4},{12,8},{16,12},{20,16},{24,20},{28,24},{0,28},{5,1},{9... | collective-permute-start | bytes 786440 | tf_op jit(solution)/shard_map/ppermute | solution.py:25
  11.9 23.6 %collective-permute-start = (bf16[512,256]{0,1:T(8,128)(2,1)S(1)}, bf16[512,256]{0,1:T(8,128)(2,1)S(1)}, u32[]{:S(2)}, u32[]{:S(2)}) collective-permute-start(bf16[512,256]{0,1:T(8,128)(2,1)S(1)} %bitcast.87), channel_id=1, source_target_pairs={{0,4},{4,8},{8,12},{12,16},{16,20},{20,24},{24,28},{28,0},{1,5},{5... | collective-permute-start | bytes 786440 | tf_op jit(solution)/shard_map/ppermute | solution.py:23
  71.8 4.0 copy-start.8
  95.4 28.8 %copy-start.26 = (s32[512]{0:T(512)S(1)}, s32[512]{0:T(512)}, u32[]{:S(2)}) copy-start(s32[512]{0:T(512)} %param.19) | copy-start | bytes 6148
  95.4 28.9 %copy-start.13 = (bf16[1,512,256]{2,1,0:T(8,128)(2,1)S(1)}, bf16[1,512,256]{2,1,0:T(8,128)(2,1)}, u32[]{:S(2)}) copy-start(bf16[1,512,256]{2,1,0:T(8,128)(2,1)} %param.14) | copy-start | bytes 786436
  121.7 12.8 %collective-permute-start.3 = (f32[512,256]{1,0:T(8,128)}, f32[512,256]{1,0:T(8,128)S(1)}, u32[]{:S(2)}, u32[]{:S(2)}) collective-permute-start(f32[512,256]{1,0:T(8,128)} %get-tuple-element.62), channel_id=1, source_target_pairs={{0,28},{4,0},{8,4},{12,8},{16,12},{20,16},{24,20},{28,24},{1,29},{... | collective-permute-start | bytes 1572872 | tf_op jit(solution)/shard_map/ppermute | solution.py:35
  122.6 12.9 %collective-permute-start.2 = (f32[512,256]{1,0:T(8,128)}, f32[512,256]{1,0:T(8,128)}, u32[]{:S(2)}, u32[]{:S(2)}) collective-permute-start(f32[512,256]{1,0:T(8,128)} %get-tuple-element.61), channel_id=1, source_target_pairs={{0,4},{4,8},{8,12},{12,16},{16,20},{20,24},{24,28},{28,0},{1,5},{5... | collective-permute-start | bytes 1572872 | tf_op jit(solution)/shard_map/ppermute | solution.py:35
  142.2 8.4 %copy-start.11 = (bf16[512,256]{1,0:T(8,128)(2,1)}, bf16[512,256]{1,0:T(8,128)(2,1)S(1)}, u32[]{:S(2)}) copy-start(bf16[512,256]{1,0:T(8,128)(2,1)S(1)} %get-tuple-element.85) | copy-start | bytes 786436
  143.5 7.1 %collective-permute-start.5 = (bf16[512,256]{1,0:T(8,128)(2,1)S(1)}, bf16[512,256]{1,0:T(8,128)(2,1)S(1)}, u32[]{:S(2)}, u32[]{:S(2)}) collective-permute-start(bf16[512,256]{1,0:T(8,128)(2,1)S(1)} %convolution_convert_fusion.1), channel_id=1, source_target_pairs={{4,0},{8,4},{12,8},{16,12},{20,16},{24,20},{28,24},{0,28},{5,1},{9... | collective-permute-start | bytes 786440 | tf_op jit(solution)/shard_map/ppermute | solution.py:25
  146.1 6.7 %collective-permute-start.4 = (bf16[512,256]{1,0:T(8,128)(2,1)S(1)}, bf16[512,256]{1,0:T(8,128)(2,1)S(1)}, u32[]{:S(2)}, u32[]{:S(2)}) collective-permute-start(bf16[512,256]{1,0:T(8,128)(2,1)S(1)} %convolution_convert_fusion.1), channel_id=1, source_target_pairs={{0,4},{4,8},{8,12},{12,16},{16,20},{20,24},{24,28},{28,0},{1,5},{5... | collective-permute-start | bytes 786440 | tf_op jit(solution)/shard_map/ppermute | solution.py:23
  173.9 5.4 copy-start.2
  173.9 5.4 copy-start.4
  184.6 7.7 %copy-start.3 = (bf16[4096,256]{1,0:T(8,128)(2,1)}, bf16[4096,256]{1,0:T(8,128)(2,1)S(1)}, u32[]{:S(2)}) copy-start(bf16[4096,256]{1,0:T(8,128)(2,1)S(1)} %get-tuple-element.83) | copy-start | bytes 6291460
  267.3 6.6 %copy-start.16 = (f32[1,512,256]{1,2,0:T(8,128)S(1)}, f32[1,512,256]{1,2,0:T(8,128)}, u32[]{:S(2)}) copy-start(f32[1,512,256]{1,2,0:T(8,128)} %get-tuple-element.65) | copy-start | bytes 1572868
  271.5 13.2 %collective-permute-start.7 = (bf16[512,256]{0,1:T(8,128)(2,1)}, bf16[512,256]{0,1:T(8,128)(2,1)S(1)}, u32[]{:S(2)}, u32[]{:S(2)}) collective-permute-start(bf16[512,256]{0,1:T(8,128)(2,1)} %get-tuple-element.64), channel_id=1, source_target_pairs={{0,28},{4,0},{8,4},{12,8},{16,12},{20,16},{24,20},{28,24},{1,29},{... | collective-permute-start | bytes 786440 | tf_op jit(solution)/shard_map/ppermute | solution.py:35
  272.6 14.0 %collective-permute-start.6 = (bf16[512,256]{0,1:T(8,128)(2,1)}, bf16[512,256]{0,1:T(8,128)(2,1)}, u32[]{:S(2)}, u32[]{:S(2)}) collective-permute-start(bf16[512,256]{0,1:T(8,128)(2,1)} %get-tuple-element.63), channel_id=1, source_target_pairs={{0,4},{4,8},{8,12},{12,16},{16,20},{20,24},{24,28},{28,0},{1,5},{5... | collective-permute-start | bytes 786440 | tf_op jit(solution)/shard_map/ppermute | solution.py:35
  274.9 11.7 %copy-start.12 = (bf16[512,256]{1,0:T(8,128)(2,1)S(1)}, bf16[512,256]{1,0:T(8,128)(2,1)}, u32[]{:S(2)}) copy-start(bf16[512,256]{1,0:T(8,128)(2,1)} %copy-done.11) | copy-start | bytes 786436
  549.6 16.8 %copy-start.17 = (f32[456,256]{1,0:T(8,128)S(1)}, f32[456,256]{1,0:T(8,128)}, u32[]{:S(2)}) copy-start(f32[456,256]{1,0:T(8,128)} %param.20) | copy-start | bytes 1400836
  549.6 16.8 %copy-start.22 = (f32[456,256]{1,0:T(8,128)S(1)}, f32[456,256]{1,0:T(8,128)}, u32[]{:S(2)}) copy-start(f32[456,256]{1,0:T(8,128)} %param.23) | copy-start | bytes 1400836
  (13 other events, 22.5 us)
Sparse Core Ops, SparseCore 0:
  203.5 325.8 all-gather.2
